TPU v7x, 512 devices: a whole 4x4x16 slice. The times are simulated.
512 devices in a mesh: dp: 4 (over x), ep: 128 (over y, z, core).
Axes of the slice: x: 4, y: 4, z: 16, core: 2. Of those that a mesh axis runs over, the one named last changes fastest.
Arguments:
- hidden_states: bfloat16 [4096, 3584], P(('dp', 'ep')), parts along dimension 0, may hold values from -120 to 120
- norm_gain: float32 [3584], replicated, may hold values from 0.1 to 1.9
- expert_ids: int32 [4096, 8], P(('dp', 'ep')), parts along dimension 0, may hold values from 0 to 15, all different within a row; in each aligned block of 8 rows (0 to 7, 8 to 15, ...) at most 5 rows name the same one
- route_scores: float32 [4096, 8], P(('dp', 'ep')), parts along dimension 0, may hold values from 0.1 to 1
- gate_weight: bfloat16 [3584, 16384], P(None, 'ep'), may hold values from -0.09375 to 0.09375
- up_weight: bfloat16 [3584, 16384], P(None, 'ep'), may hold values from -0.09375 to 0.09375
- down_weight: bfloat16 [16384, 3584], P('ep'), may hold values from -0.1875 to 0.1875
- query_latent: bfloat16 [4096, 64, 512], P(('dp', 'ep')), parts along dimension 0, may hold values from -23 to 23
- query_rope: bfloat16 [4096, 4096], P(('dp', 'ep')), parts along dimension 0, may hold values from -23 to 23
- cache_latent: bfloat16 [512, 512, 512], P(('dp', 'ep')), parts along dimension 0, may hold values from -5.3 to 5.3
- cache_rope: bfloat16 [512, 64, 512], P(('dp', 'ep')), parts along dimension 0, may hold values from -5.3 to 5.3
- tree_latent: bfloat16 [4096, 512], P(('dp', 'ep')), parts along dimension 0, may hold values from -6 to 6
- tree_rope: bfloat16 [4096, 64], P(('dp', 'ep')), parts along dimension 0, may hold values from -6 to 6
- cache_lengths: int32 [512], P(('dp', 'ep')), parts along dimension 0, may hold values from 128 to 512, as said below
- tree_parents: int32 [4096], P(('dp', 'ep')), parts along dimension 0, may hold values from 0 to 6, as said below
Outputs:
- attention_out: bfloat16 [4096, 64, 512], P(('dp', 'ep')), parts along dimension 0
- expert_out: bfloat16 [4096, 3584], P(('dp', 'ep')), parts along dimension 0
There are 4 independent parts, one for each index of `dp`. A program takes and returns all parts, laid end to end along the dimension named above; an argument that names none is the same for every part. Nothing has to cross between parts.
Inputs may be any that keep to these rules, and one draw needn't show every extreme that they name: `expert_ids`: in the 8 rows of one device each expert is named by at most 5 rows, a bound that some block reaches; each row names 8 different experts. `cache_lengths`: some request holds exactly 512 positions. `tree_parents`: counting candidates from 0 within their request, candidate i > 0 has a parent below i, and candidate 0 has 0.
All inputs are finite; a program needn't handle non-finite values.
Results may differ from a plain program's by a relative error of at most 0.008.
Values may be sent and summed in bfloat16 or wider, within the bound.
No kernel may reach another device: no remote copies, remote signals or barrier semaphores. Data moves between devices by JAX's collectives and lax.ppermute only.
A program may use at most 64 MiB of HBM per device.

v0:
```python
import jax
import jax.numpy as jnp
from jax import lax
from jax.sharding import Mesh, PartitionSpec as P

HID = 1024
EXPERTS = 16
softmax_scale = 192.0 ** (-0.5)
route_scale = 2.5
norm_eps = 1e-06
very_negative = -1e30
grid_axes = ("dp", "y", "z", "c")


def visible_tree(parents):
    tree_size = parents.shape[0]
    position = jnp.arange(tree_size, dtype=jnp.int32)
    parent_map = ((parents[:, None] == position[None, :]) & (position[:, None] > 0)).astype(
        jnp.float32
    )
    identity = jnp.eye(tree_size, dtype=jnp.float32)
    reached = identity
    for sweep_index in range(tree_size):
        reached = jnp.minimum(
            identity + jnp.dot(parent_map, reached, precision=lax.Precision.HIGHEST), 1.0
        )
    return reached > 0.5


def attend_request(
    query_latent,
    query_rope,
    cache_latent,
    cache_rope,
    tree_latent,
    tree_rope,
    cache_length,
    parents,
):
    row_count = query_latent.shape[0]
    head_count = query_latent.shape[1]
    rope_width = tree_rope.shape[1]
    query_rotary = query_rope.reshape(row_count, head_count, rope_width)
    cache_scores = jnp.einsum(
        "rhc,lc->rhl", query_latent, cache_latent, preferred_element_type=jnp.float32
    )
    cache_scores = (
        cache_scores
        + jnp.einsum("rhc,cl->rhl", query_rotary, cache_rope, preferred_element_type=jnp.float32)
    ) * softmax_scale
    candidate_tree_scores = jnp.einsum(
        "rhc,jc->rhj", query_latent, tree_latent, preferred_element_type=jnp.float32
    )
    candidate_tree_scores = (
        candidate_tree_scores
        + jnp.einsum("rhc,jc->rhj", query_rotary, tree_rope, preferred_element_type=jnp.float32)
    ) * softmax_scale
    cache_live = (jnp.arange(cache_latent.shape[0], dtype=jnp.int32) < cache_length)[None, None, :]
    tree_seen = visible_tree(parents)[:, None, :]
    cache_scores = jnp.where(cache_live, cache_scores, very_negative)
    candidate_tree_scores = jnp.where(tree_seen, candidate_tree_scores, very_negative)
    row_peak = jnp.maximum(
        jnp.max(cache_scores, axis=-1, keepdims=True),
        jnp.max(candidate_tree_scores, axis=-1, keepdims=True),
    )
    cache_exp = jnp.where(cache_live, jnp.exp(cache_scores - row_peak), 0.0)
    tree_exp = jnp.where(tree_seen, jnp.exp(candidate_tree_scores - row_peak), 0.0)
    denominator = jnp.sum(cache_exp, axis=-1, keepdims=True) + jnp.sum(
        tree_exp, axis=-1, keepdims=True
    )
    cache_probs = (cache_exp / denominator).astype(jnp.bfloat16)
    tree_probs = (tree_exp / denominator).astype(jnp.bfloat16)
    attended = jnp.einsum(
        "rhl,lc->rhc", cache_probs, cache_latent, preferred_element_type=jnp.float32
    )
    attended = attended + jnp.einsum(
        "rhj,jc->rhc", tree_probs, tree_latent, preferred_element_type=jnp.float32
    )
    return attended.astype(jnp.bfloat16)


def combine_table(expert_ids, route_scores):
    router_weight_matrix = (
        route_scale * route_scores / jnp.sum(route_scores, axis=-1, keepdims=True)
    ).astype(jnp.bfloat16)
    matches = expert_ids[:, :, None] == jnp.arange(EXPERTS, dtype=jnp.int32)[None, None, :]
    return jnp.sum(
        jnp.where(matches, router_weight_matrix.astype(jnp.float32)[:, :, None], 0.0), axis=1
    ).astype(jnp.bfloat16)


def swap_core(value):
    return lax.ppermute(value, "c", [(0, 1), (1, 0)])


def gated(rows, share, gate_weight, up_weight, down_weight):
    gate_act = jnp.dot(rows, gate_weight, preferred_element_type=jnp.float32)
    up_act = jnp.dot(rows, up_weight, preferred_element_type=jnp.float32)
    hidden = (share * jax.nn.silu(gate_act) * up_act).astype(jnp.bfloat16)
    return jnp.dot(hidden, down_weight, preferred_element_type=jnp.float32)


def local(
    hidden_states,
    norm_gain,
    expert_ids,
    route_scores,
    gate_weight,
    up_weight,
    down_weight,
    query_latent,
    query_rope,
    cache_latent,
    cache_rope,
    tree_latent,
    tree_rope,
    cache_lengths,
    tree_parents,
):
    other = [swap_core(w) for w in (gate_weight, up_weight, down_weight)]
    states = hidden_states.astype(jnp.float32)
    normed = (
        states * lax.rsqrt(jnp.mean(states * states, axis=-1, keepdims=True) + norm_eps) * norm_gain
    ).astype(jnp.bfloat16)
    width = normed.shape[1]
    combine = combine_table(expert_ids, route_scores)
    packed = jnp.concatenate([normed, jnp.pad(combine, ((0, 0), (0, 128 - EXPERTS)))], axis=1)
    gathered = lax.all_gather(packed, ("y", "z"), axis=0, tiled=True)
    attention_out = attend_request(
        query_latent,
        query_rope,
        cache_latent[0],
        cache_rope[0],
        tree_latent,
        tree_rope,
        cache_lengths[0],
        tree_parents,
    )
    chip = lax.axis_index("y") * lax.axis_size("z") + lax.axis_index("z")
    unit_count = 2 * gate_weight.shape[1]
    expert = chip * unit_count // HID
    rows = gathered[:, :width]
    shares = gathered[:, width:].astype(jnp.float32)
    share = jnp.sum(
        jnp.where(jnp.arange(shares.shape[1])[None, :] == expert, shares, 0.0),
        axis=1,
        keepdims=True,
    )
    partial = gated(rows, share, gate_weight, up_weight, down_weight) + gated(rows, share, *other)
    expert_out = lax.psum_scatter(
        partial.astype(jnp.bfloat16), ("y", "z"), scatter_dimension=0, tiled=True
    )
    return (attention_out, expert_out)


def solution(mesh):
    devices = mesh.devices.reshape(4, 4, 16, 2)
    grid = Mesh(devices, grid_axes)
    rows = P(grid_axes, None)
    ep = ("y", "z", "c")
    placed = (
        rows,
        P(),
        rows,
        rows,
        P(None, ep),
        P(None, ep),
        P(ep, None),
        P(grid_axes, None, None),
        rows,
        P(grid_axes, None, None),
        P(grid_axes, None, None),
        rows,
        rows,
        P(grid_axes),
        P(grid_axes),
    )
    return jax.shard_map(
        local,
        mesh=grid,
        in_specs=placed,
        out_specs=(P(grid_axes, None, None), rows),
        check_vma=False,
    )
```

profile of v0, /device:TPU:2, one launch (start us, length us, event | category | flops | bytes accessed | tf_op | source)
XLA Modules:
  0.0 896.7 jit_solution(6409630612788064503)
XLA Ops:
  7.2 0.0 copy-start
  7.2 0.0 all-gather.2.cloned.1.call-start
  7.2 1.0 fusion.54
  8.2 0.8 reduce_sum.57
  9.1 0.8 fusion.76
  9.8 0.9 fusion.56
  10.7 0.8 select_reduce_fusion.1
  11.5 0.6 fusion.58
  12.1 0.0 all-gather.2.cloned.1.call-update
  12.2 0.0 reduce-scatter.2.cloned.1.call-start
  12.2 1.9 collective-permute-start.1
  14.1 2.4 collective-permute-start
  16.6 1.9 collective-permute-start.2
  18.5 143.6 %all-gather.2.cloned.1.call-done = bf16[512,3712]{1,0:T(8,128)(2,1)} async-done(((bf16[8,3712]{1,0:T(8,128)(2,1)}), bf16[512,3712]{1,0:T(8,128)(2,1)}) %all-gather.2.cloned.1.call-update) | async-done | bytes 3801104 | tf_op jit(solution)/shard_map/all_gather | solution.py:128
  162.1 1.2 select_reduce_fusion
  163.2 4.1 fusion.6
  167.4 0.0 collective-permute-done.1
  167.4 0.0 copy-done.1
  167.4 2.4 fusion
  169.8 0.0 copy-done.3
  169.8 0.0 copy-done.4
  169.9 9.0 fusion.18
  178.8 0.0 collective-permute-done
  178.8 0.0 collective-permute-done.2
  178.8 10.4 %add_convert_fusion = bf16[512,3584]{1,0:T(8,128)(2,1)} fusion(f32[512,3584]{1,0:T(8,128)} %fusion.18, bf16[128,3584]{1,0:T(8,128)(2,1)} %collective-permute-done.2, f32[512,128]{1,0:T(8,128)S(1)} %fusion, bf16[3584,128]{1,0:T(8,128)(2,1)S(1)} %collective-permute-done, bf16[512,3712]{1,0:T(8,128)(2,1)} %all-gather.2.cloned.1.call-done, ...), kind=kOutput, calls=%fused_computation | convolution fusion | flops 943652864 | bytes 16779264 | tf_op jit(solution)/shard_map/dot_general | solution.py:100
  189.2 0.0 copy-start.6
  189.2 0.0 reduce-scatter.2.cloned.1.call-update
  189.2 0.0 copy-done.5
  189.2 0.2 reshape.48
  190.1 0.2 fusion.29
  190.3 0.2 fusion.28
  190.5 0.2 fusion.27
  190.7 0.2 fusion.26
  190.9 0.2 fusion.25
  191.1 0.2 fusion.24
  191.3 0.2 fusion.23
  191.5 0.2 fusion.30
  191.7 0.0 copy-done.7
  191.7 0.3 fusion.65
  192.0 0.2 fusion.99
  192.3 0.5 fusion.34
  192.8 0.0 copy-done.6
  192.8 0.4 fusion.98
  193.1 0.1 fusion.59
  193.2 0.3 fusion.31
  193.6 0.5 fusion.32
  194.1 1.2 fusion.10
  195.4 694.5 %reduce-scatter.2.cloned.1.call-done = bf16[8,3584]{1,0:T(8,128)(2,1)} async-done(((bf16[512,3584]{1,0:T(8,128)(2,1)}), bf16[8,3584]{1,0:T(8,128)(2,1)}) %reduce-scatter.2.cloned.1.call-update) | async-done | bytes 57360 | tf_op jit(solution)/shard_map/reduce_scatter | solution.py:150
  (18 shorter events, 0.1 us)
Async XLA Ops:
  7.2 185.1 %copy-start = (bf16[1,512,512]{2,1,0:T(8,128)(2,1)S(1)}, bf16[1,512,512]{2,1,0:T(8,128)(2,1)}, u32[]{:S(2)}) copy-start(bf16[1,512,512]{2,1,0:T(8,128)(2,1)} %param.24) | copy-start | bytes 1572868
  7.2 154.9 %all-gather.2.cloned.1.call-start = ((), (), s32[]{:S(2)}) async-start(), calls=%async_computation.1 | async-start | bytes 3860480 | tf_op jit(solution)/shard_map/all_gather | solution.py:128
  12.2 877.7 %reduce-scatter.2.cloned.1.call-start = ((), (), s32[]{:S(2)}) async-start(), calls=%async_computation.2 | async-start | bytes 3727360 | tf_op jit(solution)/shard_map/reduce_scatter | solution.py:150
  12.2 155.2 %collective-permute-start.1 = (bf16[3584,128]{1,0:T(8,128)(2,1)}, bf16[3584,128]{1,0:T(8,128)(2,1)}, u32[]{:S(2)}, u32[]{:S(2)}) collective-permute-start(bf16[3584,128]{1,0:T(8,128)(2,1)} %param.20), channel_id=1, source_target_pairs={{0,1},{1,0},{2,3},{3,2},{4,5},{5,4},{6,7},{7,6},{8,9},{9,8},{10,11... | collective-permute-start | bytes 2752520 | tf_op jit(solution)/shard_map/ppermute | solution.py:93
  14.1 164.7 %collective-permute-start = (bf16[3584,128]{1,0:T(8,128)(2,1)}, bf16[3584,128]{1,0:T(8,128)(2,1)S(1)}, u32[]{:S(2)}, u32[]{:S(2)}) collective-permute-start(bf16[3584,128]{1,0:T(8,128)(2,1)} %param.19), channel_id=1, source_target_pairs={{0,1},{1,0},{2,3},{3,2},{4,5},{5,4},{6,7},{7,6},{8,9},{9,8},{10,11... | collective-permute-start | bytes 2752520 | tf_op jit(solution)/shard_map/ppermute | solution.py:93
  16.6 162.3 %collective-permute-start.2 = (bf16[128,3584]{1,0:T(8,128)(2,1)}, bf16[128,3584]{1,0:T(8,128)(2,1)}, u32[]{:S(2)}, u32[]{:S(2)}) collective-permute-start(bf16[128,3584]{1,0:T(8,128)(2,1)} %param.21), channel_id=1, source_target_pairs={{0,1},{1,0},{2,3},{3,2},{4,5},{5,4},{6,7},{7,6},{8,9},{9,8},{10,11... | collective-permute-start | bytes 2752520 | tf_op jit(solution)/shard_map/ppermute | solution.py:93
  162.1 5.3 copy-start.1
  167.4 2.4 copy-start.3
  167.4 2.5 copy-start.4
  178.8 10.4 %copy-start.5 = (bf16[8,4096]{1,0:T(8,128)(2,1)S(1)}, bf16[8,4096]{1,0:T(8,128)(2,1)}, u32[]{:S(2)}) copy-start(bf16[8,4096]{1,0:T(8,128)(2,1)} %param.23) | copy-start | bytes 196612
  189.2 1.0 copy-start.9
  189.2 2.5 copy-start.2
  189.2 2.5 copy-start.7
  189.2 2.9 copy-start.8
  189.2 3.6 copy-start.6
Sparse Core Ops, SparseCore 0:
  12.3 149.7 all-gather.1
  189.3 700.4 reduce-scatter.1
where the time goes:
time: 897 us
  waiting for transfers between devices  838 us (93%)
  matrix products  30.5 us (3%)
  between operations  15 us (2%)
    reduce_scatter x1, waiting for transfers between devices, local(): lax.psum_scatter(partial.astype(jnp.bfloat16), ('y', 'z'), scatter_dimens...  695 us
    all_gather x1, waiting for transfers between devices, local(): gathered = lax.all_gather(packed, ('y', 'z'), axis=0, tiled=True)  144 us
    dot_general x2, matrix products, gated(): return jnp.dot(hidden, down_weight, preferred_element_type=jnp.float32)  19.3 us
  transfers between devices with their start and end apart: 5, of which 2 were waited for; matrix products, arithmetic and copies ran while one was open for 2% of the time, Pallas kernels for 0%

commit v1 on v0

--- a/solution.py
+++ b/solution.py
@@ -2,6 +2,7 @@
 import jax.numpy as jnp
 from jax import lax
 from jax.sharding import Mesh, PartitionSpec as P
+from jax.lax import all_to_all, axis_size
 
 HID = 1024
 EXPERTS = 16
@@ -125,7 +126,20 @@
     width = normed.shape[1]
     combine = combine_table(expert_ids, route_scores)
     packed = jnp.concatenate([normed, jnp.pad(combine, ((0, 0), (0, 128 - EXPERTS)))], axis=1)
-    gathered = lax.all_gather(packed, ("y", "z"), axis=0, tiled=True)
+
+    def _fit_loops(chunk):
+        state_now = jnp.concatenate(
+            all_to_all(
+                jnp.stack([chunk for _ in range(axis_size(("y", "z")))], 0),
+                ("y", "z"),
+                split_axis=0,
+                concat_axis=0,
+            ),
+            0,
+        )
+        return state_now
+
+    gathered = _fit_loops(packed)
     attention_out = attend_request(
         query_latent,
         query_rope,

time: 897 us -> 938 us (1.046)
  the two profiles are of different devices: /device:TPU:2 before, /device:TPU:6 now
where the time goes in v1:
time: 938 us
  waiting for transfers between devices  858 us (91%)
  matrix products  31.5 us (3%)
  starting transfers between devices  25.4 us (3%)
  between operations  15 us (2%)
    reduce_scatter x1, waiting for transfers between devices, local(): lax.psum_scatter(partial.astype(jnp.bfloat16), ('y', 'z'), scatter_dimens...  693 us
    all_to_all x1, waiting for transfers between devices, _fit_loops(): all_to_all(jnp.stack([chunk for _ in range(axis_size(('y', 'z')))], 0), (...  165 us
    dot_general x2, matrix products, gated(): return jnp.dot(hidden, down_weight, preferred_element_type=jnp.float32)  19.3 us
    all_to_all x1, starting transfers between devices, _fit_loops(): all_to_all(jnp.stack([chunk for _ in range(axis_size(('y', 'z')))], 0), (...  19.1 us
  transfers between devices with their start and end apart: 5, of which 2 were waited for; matrix products, arithmetic and copies ran while one was open for 2% of the time, Pallas kernels for 0%

profile of v1, /device:TPU:6, one launch (start us, length us, event | category | flops | bytes accessed | tf_op | source)
XLA Modules:
  0.0 938.0 jit_solution(15049975402484868074)
XLA Ops:
  7.2 0.0 copy-start
  7.2 1.0 fusion.54
  8.2 0.8 reduce_sum.57
  9.0 0.8 fusion.76
  9.8 0.9 fusion.56
  10.7 0.8 select_reduce_fusion.1
  11.5 2.1 stack.2
  13.6 19.1 %all-to-all-start = ((bf16[64,8,3712]{2,1,0:T(8,128)(2,1)}), bf16[64,8,3712]{2,1,0:T(8,128)(2,1)}, u32[]{:S(2)}, u32[]{:S(2)}) async-start(bf16[64,8,3712]{2,1,0:T(8,128)(2,1)} %stack.2), calls=%async_computation | async-start | bytes 7602176 | tf_op jit(solution)/shard_map/all_to_all | solution.py:132
  32.7 0.0 reduce-scatter.2.cloned.1.call-start
  32.7 0.0 copy-done.2
  32.7 1.9 collective-permute-start.1
  34.7 2.4 collective-permute-start
  37.1 0.0 copy-done.3
  37.1 1.9 collective-permute-start.2
  39.0 164.9 %all-to-all-done = bf16[64,8,3712]{2,1,0:T(8,128)(2,1)} async-done(((bf16[64,8,3712]{2,1,0:T(8,128)(2,1)}), bf16[64,8,3712]{2,1,0:T(8,128)(2,1)}, u32[]{:S(2)}, u32[]{:S(2)}) %all-to-all-start) | async-done | bytes 3801120 | tf_op jit(solution)/shard_map/all_to_all | solution.py:132
  203.9 1.0 select_reduce_fusion
  204.9 4.1 fusion.6
  209.0 0.0 collective-permute-done.1
  209.0 3.4 fusion
  212.4 9.0 fusion.18
  221.4 0.0 collective-permute-done
  221.4 0.0 collective-permute-done.2
  221.4 10.4 %add_convert_fusion = bf16[512,3584]{1,0:T(8,128)(2,1)} fusion(f32[512,3584]{1,0:T(8,128)} %fusion.18, bf16[128,3584]{1,0:T(8,128)(2,1)} %collective-permute-done.2, f32[512,128]{1,0:T(8,128)S(1)} %fusion, bf16[3584,128]{1,0:T(8,128)(2,1)S(1)} %collective-permute-done, bf16[512,3712]{1,0:T(8,128)(2,1)} %bitcast.7, f32[512]{0:T(512)S(1)} %select_reduce_fusion), kind=kOutput, calls=%fused_computation | convolution fusion | flops 943652864 | bytes 16779264 | tf_op jit(solution)/shard_map/dot_general | solution.py:101
  231.8 0.0 copy-start.5
  231.8 0.0 reduce-scatter.2.cloned.1.call-update
  231.8 0.0 copy-done.4
  231.8 0.2 reshape.53
  232.7 0.0 copy-done.8
  232.7 0.2 fusion.29
  232.9 0.2 fusion.28
  233.1 0.2 fusion.27
  233.3 0.2 fusion.26
  233.5 0.2 fusion.25
  233.7 0.2 fusion.24
  233.9 0.2 fusion.23
  234.1 0.2 fusion.30
  234.3 0.0 copy-done.1
  234.3 0.0 copy-done.6
  234.3 0.3 fusion.65
  234.6 0.2 fusion.99
  234.9 0.0 copy-done
  234.9 0.5 fusion.34
  235.4 0.4 fusion.98
  235.7 0.1 fusion.59
  235.8 0.4 fusion.31
  236.2 0.5 fusion.32
  236.7 1.2 fusion.10
  238.0 693.2 %reduce-scatter.2.cloned.1.call-done = bf16[8,3584]{1,0:T(8,128)(2,1)} async-done(((bf16[512,3584]{1,0:T(8,128)(2,1)}), bf16[8,3584]{1,0:T(8,128)(2,1)}) %reduce-scatter.2.cloned.1.call-update) | async-done | bytes 57360 | tf_op jit(solution)/shard_map/reduce_scatter | solution.py:164
  (16 shorter events, 0.1 us)
Async XLA Ops:
  7.2 227.7 %copy-start = (bf16[1,512,512]{2,1,0:T(8,128)(2,1)S(1)}, bf16[1,512,512]{2,1,0:T(8,128)(2,1)}, u32[]{:S(2)}) copy-start(bf16[1,512,512]{2,1,0:T(8,128)(2,1)} %param.24) | copy-start | bytes 1572868
  13.6 19.2 %copy-start.2 = (bf16[3584,128]{1,0:T(8,128)(2,1)S(1)}, bf16[3584,128]{1,0:T(8,128)(2,1)}, u32[]{:S(2)}) copy-start(bf16[3584,128]{1,0:T(8,128)(2,1)} %param.20) | copy-start | bytes 2752516
  13.6 23.5 %copy-start.3 = (bf16[128,3584]{1,0:T(8,128)(2,1)S(1)}, bf16[128,3584]{1,0:T(8,128)(2,1)}, u32[]{:S(2)}) copy-start(bf16[128,3584]{1,0:T(8,128)(2,1)} %param.21) | copy-start | bytes 2752516
  13.6 190.3 %all-to-all-start = ((bf16[64,8,3712]{2,1,0:T(8,128)(2,1)}), bf16[64,8,3712]{2,1,0:T(8,128)(2,1)}, u32[]{:S(2)}, u32[]{:S(2)}) async-start(bf16[64,8,3712]{2,1,0:T(8,128)(2,1)} %stack.2), calls=%async_computation | async-start | bytes 7602176 | tf_op jit(solution)/shard_map/all_to_all | solution.py:132
  32.7 898.5 %reduce-scatter.2.cloned.1.call-start = ((), (), s32[]{:S(2)}) async-start(), calls=%async_computation.2 | async-start | bytes 3727360 | tf_op jit(solution)/shard_map/reduce_scatter | solution.py:164
  32.7 176.3 %collective-permute-start.1 = (bf16[3584,128]{1,0:T(8,128)(2,1)S(1)}, bf16[3584,128]{1,0:T(8,128)(2,1)}, u32[]{:S(2)}, u32[]{:S(2)}) collective-permute-start(bf16[3584,128]{1,0:T(8,128)(2,1)S(1)} %copy-done.2), channel_id=1, source_target_pairs={{0,1},{1,0},{2,3},{3,2},{4,5},{5,4},{6,7},{7,6},{8,9},{9,8},{10,11... | collective-permute-start | bytes 2752520 | tf_op jit(solution)/shard_map/ppermute | solution.py:94
  34.7 186.7 %collective-permute-start = (bf16[3584,128]{1,0:T(8,128)(2,1)}, bf16[3584,128]{1,0:T(8,128)(2,1)S(1)}, u32[]{:S(2)}, u32[]{:S(2)}) collective-permute-start(bf16[3584,128]{1,0:T(8,128)(2,1)} %param.19), channel_id=1, source_target_pairs={{0,1},{1,0},{2,3},{3,2},{4,5},{5,4},{6,7},{7,6},{8,9},{9,8},{10,11... | collective-permute-start | bytes 2752520 | tf_op jit(solution)/shard_map/ppermute | solution.py:94
  37.1 184.3 %collective-permute-start.2 = (bf16[128,3584]{1,0:T(8,128)(2,1)S(1)}, bf16[128,3584]{1,0:T(8,128)(2,1)}, u32[]{:S(2)}, u32[]{:S(2)}) collective-permute-start(bf16[128,3584]{1,0:T(8,128)(2,1)S(1)} %copy-done.3), channel_id=1, source_target_pairs={{0,1},{1,0},{2,3},{3,2},{4,5},{5,4},{6,7},{7,6},{8,9},{9,8},{10,11... | collective-permute-start | bytes 2752520 | tf_op jit(solution)/shard_map/ppermute | solution.py:94
  221.4 10.4 %copy-start.4 = (bf16[8,4096]{1,0:T(8,128)(2,1)S(1)}, bf16[8,4096]{1,0:T(8,128)(2,1)}, u32[]{:S(2)}) copy-start(bf16[8,4096]{1,0:T(8,128)(2,1)} %param.23) | copy-start | bytes 196612
  231.8 1.0 copy-start.8
  231.8 2.5 copy-start.1
  231.8 2.5 copy-start.6
  231.8 2.9 copy-start.7
  231.8 3.6 copy-start.5
Sparse Core Ops, SparseCore 0:
  231.9 699.1 reduce-scatter.1
